TPU v7x, 512 devices: a whole 4x8x8 slice. The times are simulated.
512 devices in a mesh: pitch: 32 (over x, z), span: 8 (over y), row: 2 (over core).
Axes of the slice: x: 4, y: 8, z: 8, core: 2. Of those that a mesh axis runs over, the one named last changes fastest.
Arguments:
- fields: float32 [3, 512, 128, 512], P(None, 'pitch', 'span', 'row'), may hold values from -6 to 6
- diffusivity: float32 [512, 128, 512], P('pitch', 'span', 'row'), may hold values from 0.01 to 0.1
- mean_flow: bfloat16 [128, 2, 512], P('span', None, 'row'), may hold values from -6 to 6
- radial_kernel: bfloat16 [128, 128], replicated
- tracer_values: float32 [10, 1048576], P(None, ('pitch', 'span', 'row')), may hold values from -6 to 6
- tracer_cells: int32 [1048576], P(('pitch', 'span', 'row')), may hold values from 0 to 65535
- tracer_dest: int32 [1048576, 1], P(('pitch', 'span', 'row')), may hold values from 0 to 31; in each aligned block of 2048 rows (0 to 2047, 2048 to 4095, ...) at most 128 rows name the same one
- interface_map: int32 [2, 512], P('row', 'pitch'), may hold values from 0 to 511, as said below
Outputs:
- advected: float32 [3, 512, 128, 512], P(None, 'pitch', 'span', 'row')
- arrived: float32 [10, 2097152], P(None, ('pitch', 'span', 'row'))
Inputs may be any that keep to these rules, and one draw needn't show every extreme that they name: `tracer_cells`: the local index of the owning cell within the block of the device that holds the tracer, i * 16 * 256 + r * 256 + a for local indices i, r, a. `tracer_dest`: at most 128 of the tracers of one device go to one pitch index. `interface_map`: for one offset o of each draw, row 0 holds (i + o) mod 512 and row 1 holds (i - o) mod 512, so the two rows are inverse permutations.
All inputs are finite; a program needn't handle non-finite values.
Results may differ from a plain program's by a relative error of at most 0.0015.
Values may be sent and summed in bfloat16 or wider, within the bound.
A program may use at most 128 MiB of HBM per device.

v0:
```python
import jax
import jax.numpy as jnp
from jax import lax
from jax.sharding import PartitionSpec as P

SUB = 2
TIME_STEP = 0.9
AXIAL_SPEED = 0.15
PITCH_SPEED = 0.15


def swapped(block, axis, apart):
    count = lax.axis_size(axis)
    route = []
    for low in range(count):
        high = low | 1 << apart
        if high != low and high < count:
            route += [(low, high), (high, low)]
    return lax.ppermute(block, axis, route)


def padded(cells, sides, width):
    for axis, dim in sides:
        count = lax.axis_size(axis)
        head = lax.slice_in_dim(cells, 0, width, axis=dim)
        tail = lax.slice_in_dim(cells, cells.shape[dim] - width, cells.shape[dim], axis=dim)
        cells = jnp.concatenate(
            [
                lax.ppermute(tail, axis, [(i, (i + 1) % count) for i in range(count)]),
                cells,
                lax.ppermute(head, axis, [((i + 1) % count, i) for i in range(count)]),
            ],
            axis=dim,
        )
    return cells


def face_flux(left_values, right_values, left_kappa, right_kappa, face_speed):
    diffusion = -0.5 * (left_kappa + right_kappa) * (right_values - left_values)
    if face_speed is None:
        return diffusion
    return (
        jnp.maximum(face_speed, 0.0) * left_values
        + jnp.minimum(face_speed, 0.0) * right_values
        + diffusion
    )


def interface_ghost(own_face, local_map):
    across = swapped(own_face, "row", 0)
    picked = lax.all_gather(across, "pitch", axis=1, tiled=True)
    return jnp.take(picked, local_map, axis=1)


def update_core(extended, speed_axial, speed_pitch, ghost_face, wall_mask, row_id):
    along_pitch = extended[:, :, 1:-1, :]
    pitch_flux = face_flux(
        along_pitch[:3, :-1],
        along_pitch[:3, 1:],
        along_pitch[3, :-1],
        along_pitch[3, 1:],
        speed_pitch,
    )
    along_radius = extended[:, 1:-1]
    radial_flux = (
        face_flux(
            along_radius[:3, :, :-1],
            along_radius[:3, :, 1:],
            along_radius[3, :, :-1],
            along_radius[3, :, 1:],
            None,
        )
        * wall_mask[:, None]
    )
    core = extended[:, 1:-1, 1:-1]
    pitch_cells = core.shape[1]
    full_stack = jnp.concatenate(
        [core, jnp.broadcast_to(speed_axial[None, None], (1, pitch_cells) + speed_axial.shape)], 0
    )
    upstream = jnp.where(row_id == 0, full_stack[..., 0], ghost_face)
    downstream = jnp.where(row_id == 0, ghost_face, full_stack[..., -1])
    line = jnp.concatenate([upstream[..., None], full_stack, downstream[..., None]], -1)
    face_speed = 0.5 * (line[4, ..., :-1] + line[4, ..., 1:])
    axial_flux = face_flux(
        line[:3, ..., :-1], line[:3, ..., 1:], line[3, ..., :-1], line[3, ..., 1:], face_speed
    )
    divergence = (
        pitch_flux[:, 1:]
        - pitch_flux[:, :-1]
        + radial_flux[:, :, 1:]
        - radial_flux[:, :, :-1]
        + axial_flux[..., 1:]
        - axial_flux[..., :-1]
    )
    return core[:3] - TIME_STEP * divergence


def advance(state, diffusivity, speed_axial, speed_pitch, local_map, wall_mask):
    pitch_cells = state.shape[1]
    stacked = jnp.concatenate([state, diffusivity[None]], 0)
    extended = padded(stacked, (("pitch", 1), ("span", 2)), 1)
    full_stack = jnp.concatenate(
        [stacked, jnp.broadcast_to(speed_axial[None, None], (1, pitch_cells) + speed_axial.shape)],
        0,
    )
    row_id = lax.axis_index("row")
    own_face = jnp.where(row_id == 0, full_stack[..., -1], full_stack[..., 0])
    ghost_face = interface_ghost(own_face, local_map)
    return update_core(extended, speed_axial, speed_pitch, ghost_face, wall_mask, row_id)


def local(
    fields,
    diffusivity,
    mean_flow,
    radial_kernel,
    tracer_values,
    tracer_cells,
    tracer_dest,
    interface_map,
):
    radial_cells = mean_flow.shape[0]
    axial_cells = mean_flow.shape[2]
    flat_width = 2 * axial_cells
    span_id = lax.axis_index("span")
    kernel_cols = lax.dynamic_slice_in_dim(radial_kernel, span_id * radial_cells, radial_cells, 1)
    flat_rows = mean_flow.reshape(radial_cells, flat_width)
    smoothed = lax.psum_scatter(
        jnp.dot(kernel_cols, flat_rows, preferred_element_type=jnp.float32),
        "span",
        scatter_dimension=0,
        tiled=True,
    )
    smoothed = smoothed.reshape(radial_cells, 2, axial_cells)
    speed_axial = AXIAL_SPEED * (1.0 + 0.5 * jnp.tanh(smoothed[:, 0]))
    speed_pitch = PITCH_SPEED * jnp.tanh(smoothed[:, 1])
    plane_size = radial_cells * axial_cells
    sample_fields = jnp.take(fields.reshape(fields.shape[0], -1), tracer_cells, axis=1)
    sample_speed = jnp.take(
        jnp.stack([speed_axial, speed_pitch]).reshape(2, plane_size),
        tracer_cells % plane_size,
        axis=1,
    )
    sampled = jnp.concatenate([sample_fields, sample_speed], 0)
    head_rows = tracer_values[:5]
    tail_rows = tracer_values[5:]
    updated = jnp.concatenate(
        [head_rows + 0.5 * (sampled - head_rows), tail_rows + 0.8 * sampled], 0
    )
    npitch = lax.axis_size("pitch")
    capacity = 2 * tracer_values.shape[1] // npitch
    targets = tracer_dest[:, 0]
    onehot = (targets[:, None] == jnp.arange(npitch, dtype=jnp.int32)[None]).astype(jnp.int32)
    slot_index = jnp.sum((jnp.cumsum(onehot, 0) - onehot) * onehot, 1)
    position = targets * capacity + slot_index
    outgoing = (
        jnp.zeros((tracer_values.shape[0], npitch * capacity), jnp.float32)
        .at[:, position]
        .set(updated)
    )
    arrived = lax.all_to_all(outgoing, "pitch", split_axis=1, concat_axis=1, tiled=True)
    face_index = span_id * radial_cells + jnp.arange(radial_cells + 1, dtype=jnp.int32)
    total_radial = radial_cells * lax.axis_size("span")
    wall_mask = ((face_index > 0) & (face_index < total_radial)).astype(jnp.float32)
    local_map = interface_map[0]
    current = fields
    for substep in range(SUB):
        current = advance(current, diffusivity, speed_axial, speed_pitch, local_map, wall_mask)
    return (current, arrived)


def solution(mesh):
    placed = (
        P(None, "pitch", "span", "row"),
        P("pitch", "span", "row"),
        P("span", None, "row"),
        P(),
        P(None, ("pitch", "span", "row")),
        P(("pitch", "span", "row")),
        P(("pitch", "span", "row"), None),
        P("row", "pitch"),
    )
    return jax.shard_map(
        local,
        mesh=mesh,
        in_specs=placed,
        out_specs=(P(None, "pitch", "span", "row"), P(None, ("pitch", "span", "row"))),
        check_vma=False,
    )
```

profile of v0, /device:TPU:24, one launch (start us, length us, event | category | flops | bytes accessed | tf_op | source)
XLA Modules:
  0.0 287.4 jit_solution(10924218289385498217)
XLA Ops:
  7.2 1.1 copy.928
  8.4 1.3 constant_dynamic-update-slice_fusion
  9.8 0.7 fusion.65
  10.5 4.3 %collective-permute-start = (f32[4,1,16,256]{3,2,1,0:T(8,128)}, f32[4,1,16,256]{3,2,1,0:T(8,128)S(1)}, u32[]{:S(2)}, u32[]{:S(2)}) collective-permute-start(f32[4,1,16,256]{3,2,1,0:T(8,128)} %get-tuple-element.57), channel_id=1, source_target_pairs={{0,16},{16,32},{32,48},{48,64},{64,80},{80,96},{96,112},{112,128},... | collective-permute-start | bytes 196616 | tf_op jit(solution)/shard_map/ppermute | solution.py:29
  14.7 10.8 %collective-permute-start.1 = (f32[4,1,16,256]{3,2,1,0:T(8,128)}, f32[4,1,16,256]{3,2,1,0:T(8,128)}, u32[]{:S(2)}, u32[]{:S(2)}) collective-permute-start(f32[4,1,16,256]{3,2,1,0:T(8,128)} %get-tuple-element.58), channel_id=1, source_target_pairs={{16,0},{32,16},{48,32},{64,48},{80,64},{96,80},{112,96},{128,112},... | collective-permute-start | bytes 196616 | tf_op jit(solution)/shard_map/ppermute | solution.py:31
  25.6 0.9 fusion.48
  27.0 0.7 compare_and_fusion.2
  27.7 16.7 %copy.818 = f32[3,16,16,256]{0,3,2,1:T(8,128)} copy(f32[3,16,16,256]{3,2,1,0:T(8,128)S(1)} %copy-done.2) | data formatting | bytes 1572864 | tf_op args[0]
  44.4 18.2 %gather_fusion = f32[2048,3]{1,0:T(8,128)} fusion(f32[3,65536]{0,1:T(8,128)} %bitcast.121, s32[2048]{0:T(1024)S(1)} %get-tuple-element.74), kind=kCustom, calls=%fused_computation.2 | custom fusion | bytes 57344 | tf_op jit(solution)/shard_map/jit(_take)/gather | solution.py:138
  62.6 2.6 select_bitcast_fusion.1
  65.2 2.2 copy.820
  67.3 9.1 %reduce-window.6 = s32[32,16,128]{2,1,0:T(8,128)S(1)} reduce-window(s32[32,16,128]{2,1,0:T(8,128)S(1)} %fusion.43, s32[]{:T(128)} %constant.30.clone.1), window={size=1x1x128 pad=0_0x0_0x127_0}, to_apply=%region_1.0 | reduce-window | flops 8323072 | bytes 524292 | tf_op jit(solution)/shard_map/reduce-window
  77.9 0.9 pad_maximum_fusion.12
  79.0 4.7 %collective-permute-start.2 = (f32[4,18,1,256]{3,0,2,1:T(4,128)S(1)}, f32[4,18,1,256]{3,0,2,1:T(4,128)S(1)}, u32[]{:S(2)}, u32[]{:S(2)}) collective-permute-start(f32[4,18,1,256]{3,0,2,1:T(4,128)S(1)} %copy.846), channel_id=1, source_target_pairs={{0,2},{2,4},{4,6},{6,8},{8,10},{10,12},{12,14},{14,0},{1,3},{3,5},... | collective-permute-start | bytes 221192 | tf_op jit(solution)/shard_map/ppermute | solution.py:29
  83.7 1.9 collective-permute-start.3
  85.7 2.2 fusion.14
  87.9 0.7 fusion.39
  88.6 0.9 copy.769
  89.6 0.7 copy_dynamic-update-slice_fusion.2
  90.3 0.9 collective-permute-done.3
  91.3 1.2 fusion.19
  92.5 0.8 reshape.138
  93.7 0.8 copy.826
  94.6 0.8 copy.827
  95.4 0.7 bitcast_select_fusion.5
  96.1 1.9 collective-permute-start.4
  98.1 0.6 copy.819
  98.8 7.6 %gather_fusion.1 = f32[2048,2]{1,0:T(8,128)} fusion(f32[2,4096]{0,1:T(8,128)S(1)} %copy.819, s32[2048]{0:T(1024)S(1)} %get-tuple-element.75), kind=kCustom, calls=%fused_computation.3 | custom fusion | bytes 40960 | tf_op jit(solution)/shard_map/jit(_take)/gather | solution.py:139
  106.4 1.6 select_bitcast_fusion
  108.4 1.3 copy.822
  109.8 6.5 %scatter_custom_fusion = f32[10,4096]{0,1:T(8,128)S(1)} fusion(s32[2048]{0:T(1024)} %bitcast.141, f32[2048,10]{1,0:T(8,128)} %copy.822, f32[]{:T(128)} %constant.45.clone.1), kind=kCustom, calls=%fused_computation.51 | custom fusion | bytes 164352 | tf_op jit(solution)/shard_map/scatter | solution.py:159
  116.2 1.3 copy.823
  117.6 5.2 %all-to-all-start = ((f32[10,32,128]{2,0,1:T(8,128)}), f32[10,32,128]{2,0,1:T(8,128)}, u32[]{:S(2)}, u32[]{:S(2)}) async-start(f32[10,32,128]{2,0,1:T(8,128)} %copy.823), calls=%async_computation.1 | async-start | bytes 524288 | tf_op jit(solution)/shard_map/all_to_all | solution.py:161
  122.8 2.5 fusion.5
  125.3 0.8 copy.782
  126.2 51.2 %all_gather.6 = f32[5,512,16]{2,1,0:T(8,128)S(1)} all-gather(f32[5,16,16]{2,1,0:T(8,128)S(1)} %copy.782), channel_id=1, replica_groups=mesh['pitch'=32,'span'=8,'row'=2] {'pitch'}, dimensions={1}, use_global_device_ids=true | all-gather | bytes 168960 | tf_op jit(solution)/shard_map/all_gather | solution.py:51
  177.3 2.2 copy.783
  179.5 2.8 gather_fusion.2
  182.4 1.5 fusion.46
  183.9 2.2 copy.786
  186.1 1.4 copy.789
  187.5 2.0 fusion.2
  189.9 0.9 copy-done.5
  190.8 0.8 fusion.23
  192.4 1.0 fusion.60
  193.4 1.9 copy.834
  195.3 0.8 copy.835
  196.2 1.9 collective-permute-start.9
  198.1 0.6 fusion.64
  198.8 2.7 collective-permute-start.5
  201.4 6.5 %collective-permute-start.6 = (f32[4,1,16,256]{3,2,1,0:T(8,128)S(1)}, f32[4,1,16,256]{3,2,1,0:T(8,128)S(1)}, u32[]{:S(2)}, u32[]{:S(2)}) collective-permute-start(f32[4,1,16,256]{3,2,1,0:T(8,128)S(1)} %get-tuple-element.54), channel_id=1, source_target_pairs={{16,0},{32,16},{48,32},{64,48},{80,64},{96,80},{112,96},{128,112},... | collective-permute-start | bytes 196616 | tf_op jit(solution)/shard_map/ppermute | solution.py:31
  208.0 47.9 %all_gather.7 = f32[5,512,16]{2,1,0:T(8,128)S(1)} all-gather(f32[5,16,16]{2,1,0:T(8,128)S(1)} %copy.807), channel_id=1, replica_groups=mesh['pitch'=32,'span'=8,'row'=2] {'pitch'}, dimensions={1}, use_global_device_ids=true | all-gather | bytes 168960 | tf_op jit(solution)/shard_map/all_gather | solution.py:51
  255.8 2.2 copy.808
  258.0 2.1 gather_fusion.3
  260.8 1.4 copy.814
  262.2 1.8 fusion.3
  264.8 4.3 %collective-permute-start.7 = (f32[4,18,1,256]{3,0,2,1:T(4,128)S(1)}, f32[4,18,1,256]{3,0,2,1:T(4,128)S(1)}, u32[]{:S(2)}, u32[]{:S(2)}) collective-permute-start(f32[4,18,1,256]{3,0,2,1:T(4,128)S(1)} %copy.851), channel_id=1, source_target_pairs={{0,2},{2,4},{4,6},{6,8},{8,10},{10,12},{12,14},{14,0},{1,3},{3,5},... | collective-permute-start | bytes 221192 | tf_op jit(solution)/shard_map/ppermute | solution.py:29
  269.0 2.1 collective-permute-start.8
  271.4 1.0 fusion.8
  272.5 0.7 copy_dynamic-update-slice_fusion
  273.2 3.3 %collective-permute-done.8 = f32[4,18,1,256]{3,0,2,1:T(4,128)S(1)} collective-permute-done((f32[4,18,1,256]{3,0,2,1:T(4,128)S(1)}, f32[4,18,1,256]{3,0,2,1:T(4,128)S(1)}, u32[]{:S(2)}, u32[]{:S(2)}) %collective-permute-start.8) | collective-permute-done | bytes 73760 | tf_op jit(solution)/shard_map/ppermute | solution.py:31
  277.4 1.3 copy.825
  278.7 1.0 copy.824
  279.7 0.9 copy.857
  (102 shorter events, 7.0 us)
Async XLA Ops:
  7.2 18.4 %copy-start = (bf16[128,128]{1,0:T(8,128)(2,1)S(1)}, bf16[128,128]{1,0:T(8,128)(2,1)}, u32[]{:S(2)}) copy-start(bf16[128,128]{1,0:T(8,128)(2,1)} %param.13) | copy-start | bytes 98308
  7.2 85.3 %reduce-scatter.2.cloned.1.call-start = ((), (), s32[]{:S(2)}) async-start(), calls=%async_computation.2 | async-start | bytes 294912 | tf_op jit(solution)/shard_map/reduce_scatter | solution.py:128
  8.3 17.2 %copy-start.12 = (bf16[16,2,256]{2,1,0:T(2,128)(2,1)S(1)}, bf16[16,2,256]{2,1,0:T(2,128)(2,1)}, u32[]{:S(2)}) copy-start(bf16[16,2,256]{2,1,0:T(2,128)(2,1)} %param.12) | copy-start | bytes 49156
  8.3 18.2 %copy-start.2 = (f32[3,16,16,256]{3,2,1,0:T(8,128)S(1)}, f32[3,16,16,256]{3,2,1,0:T(8,128)}, u32[]{:S(2)}) copy-start(f32[3,16,16,256]{3,2,1,0:T(8,128)} %param.10) | copy-start | bytes 2359300
  9.8 17.2 %copy-start.16 = (s32[1,16]{1,0:T(1,128)S(1)}, s32[1,16]{1,0:T(1,128)}, u32[]{:S(2)}) copy-start(s32[1,16]{1,0:T(1,128)} %param.17) | copy-start | bytes 196
  9.8 17.9 %copy-start.11 = (s32[2048]{0:T(1024)S(1)}, s32[2048]{0:T(1024)}, u32[]{:S(2)}) copy-start(s32[2048]{0:T(1024)} %param.15) | copy-start | bytes 24580
  10.5 67.4 %collective-permute-start = (f32[4,1,16,256]{3,2,1,0:T(8,128)}, f32[4,1,16,256]{3,2,1,0:T(8,128)S(1)}, u32[]{:S(2)}, u32[]{:S(2)}) collective-permute-start(f32[4,1,16,256]{3,2,1,0:T(8,128)} %get-tuple-element.57), channel_id=1, source_target_pairs={{0,16},{16,32},{32,48},{48,64},{64,80},{80,96},{96,112},{112,128},... | collective-permute-start | bytes 196616 | tf_op jit(solution)/shard_map/ppermute | solution.py:29
  14.7 63.1 %collective-permute-start.1 = (f32[4,1,16,256]{3,2,1,0:T(8,128)}, f32[4,1,16,256]{3,2,1,0:T(8,128)}, u32[]{:S(2)}, u32[]{:S(2)}) collective-permute-start(f32[4,1,16,256]{3,2,1,0:T(8,128)} %get-tuple-element.58), channel_id=1, source_target_pairs={{16,0},{32,16},{48,32},{64,48},{80,64},{96,80},{112,96},{128,112},... | collective-permute-start | bytes 196616 | tf_op jit(solution)/shard_map/ppermute | solution.py:31
  27.0 66.3 %copy-start.3 = (f32[3,16,16,256]{3,1,2,0:T(8,128)}, f32[3,16,16,256]{3,1,2,0:T(8,128)S(1)}, u32[]{:S(2)}) copy-start(f32[3,16,16,256]{3,1,2,0:T(8,128)S(1)} %copy.791) | copy-start | bytes 2359300
  62.6 4.7 %copy-start.10 = (s32[2048,1]{0,1:T(1,128)S(1)}, s32[2048,1]{0,1:T(1,128)}, u32[]{:S(2)}) copy-start(s32[2048,1]{0,1:T(1,128)} %param.16) | copy-start | bytes 24580
  77.9 13.4 %copy-start.13 = (f32[17]{0:T(128)}, f32[17]{0:T(128)S(1)}, u32[]{:S(2)}) copy-start(f32[17]{0:T(128)S(1)} %and_convert_fusion) | copy-start | bytes 208
  79.0 10.6 %collective-permute-start.2 = (f32[4,18,1,256]{3,0,2,1:T(4,128)S(1)}, f32[4,18,1,256]{3,0,2,1:T(4,128)S(1)}, u32[]{:S(2)}, u32[]{:S(2)}) collective-permute-start(f32[4,18,1,256]{3,0,2,1:T(4,128)S(1)} %copy.846), channel_id=1, source_target_pairs={{0,2},{2,4},{4,6},{6,8},{8,10},{10,12},{12,14},{14,0},{1,3},{3,5},... | collective-permute-start | bytes 221192 | tf_op jit(solution)/shard_map/ppermute | solution.py:29
  83.7 7.5 %collective-permute-start.3 = (f32[4,18,1,256]{3,0,2,1:T(4,128)S(1)}, f32[4,18,1,256]{3,0,2,1:T(4,128)S(1)}, u32[]{:S(2)}, u32[]{:S(2)}) collective-permute-start(f32[4,18,1,256]{3,0,2,1:T(4,128)S(1)} %copy.847), channel_id=1, source_target_pairs={{2,0},{4,2},{6,4},{8,6},{10,8},{12,10},{14,12},{0,14},{3,1},{5,3},... | collective-permute-start | bytes 221192 | tf_op jit(solution)/shard_map/ppermute | solution.py:31
  95.4 2.7 copy-start.6
  96.1 29.2 %collective-permute-start.4 = (f32[5,16,16]{2,0,1:T(8,128)}, f32[5,16,16]{2,0,1:T(8,128)}, u32[]{:S(2)}, u32[]{:S(2)}) collective-permute-start(f32[5,16,16]{2,0,1:T(8,128)} %bitcast_select_fusion.5), channel_id=1, source_target_pairs={{0,1},{1,0},{2,3},{3,2},{4,5},{5,4},{6,7},{7,6},{8,9},{9,8},{10,11... | collective-permute-start | bytes 15368 | tf_op jit(solution)/shard_map/ppermute | solution.py:19
  106.4 1.9 copy-start.8
  106.4 1.9 copy-start.9
  117.6 161.1 %all-to-all-start = ((f32[10,32,128]{2,0,1:T(8,128)}), f32[10,32,128]{2,0,1:T(8,128)}, u32[]{:S(2)}, u32[]{:S(2)}) async-start(f32[10,32,128]{2,0,1:T(8,128)} %copy.823), calls=%async_computation.1 | async-start | bytes 524288 | tf_op jit(solution)/shard_map/all_to_all | solution.py:161
  177.3 5.0 %copy-start.7 = (f32[5,16,16,1]{2,0,1,3:T(8,128)S(1)}, f32[5,16,16,1]{2,0,1,3:T(8,128)}, u32[]{:S(2)}) copy-start(f32[5,16,16,1]{2,0,1,3:T(8,128)} %copy-done.6) | copy-start | bytes 15364
  177.3 5.0 %copy-start.15 = (pred[16]{0:T(512)(128)(4,1)S(1)}, pred[16]{0:T(512)(128)(4,1)}, u32[]{:S(2)}) copy-start(pred[16]{0:T(512)(128)(4,1)} %compare_and_fusion.2) | copy-start | bytes 52
  179.5 8.0 %copy-start.4 = (f32[3,16,16,256]{3,1,2,0:T(8,128)S(1)}, f32[3,16,16,256]{3,1,2,0:T(8,128)}, u32[]{:S(2)}) copy-start(f32[3,16,16,256]{3,1,2,0:T(8,128)} %copy-done.3) | copy-start | bytes 2359300
  189.6 1.2 copy-start.5
  196.2 11.7 %collective-permute-start.9 = (f32[5,16,16]{2,0,1:T(8,128)S(1)}, f32[5,16,16]{2,0,1:T(8,128)S(1)}, u32[]{:S(2)}, u32[]{:S(2)}) collective-permute-start(f32[5,16,16]{2,0,1:T(8,128)S(1)} %bitcast_select_fusion.2), channel_id=1, source_target_pairs={{0,1},{1,0},{2,3},{3,2},{4,5},{5,4},{6,7},{7,6},{8,9},{9,8},{10,11... | collective-permute-start | bytes 15368 | tf_op jit(solution)/shard_map/ppermute | solution.py:19
  198.8 65.5 %collective-permute-start.5 = (f32[4,1,16,256]{3,2,1,0:T(8,128)}, f32[4,1,16,256]{3,2,1,0:T(8,128)S(1)}, u32[]{:S(2)}, u32[]{:S(2)}) collective-permute-start(f32[4,1,16,256]{3,2,1,0:T(8,128)} %get-tuple-element.53), channel_id=1, source_target_pairs={{0,16},{16,32},{32,48},{48,64},{64,80},{80,96},{96,112},{112,128},... | collective-permute-start | bytes 196616 | tf_op jit(solution)/shard_map/ppermute | solution.py:29
  201.4 62.9 %collective-permute-start.6 = (f32[4,1,16,256]{3,2,1,0:T(8,128)S(1)}, f32[4,1,16,256]{3,2,1,0:T(8,128)S(1)}, u32[]{:S(2)}, u32[]{:S(2)}) collective-permute-start(f32[4,1,16,256]{3,2,1,0:T(8,128)S(1)} %get-tuple-element.54), channel_id=1, source_target_pairs={{16,0},{32,16},{48,32},{64,48},{80,64},{96,80},{112,96},{128,112},... | collective-permute-start | bytes 196616 | tf_op jit(solution)/shard_map/ppermute | solution.py:31
  264.8 7.7 %collective-permute-start.7 = (f32[4,18,1,256]{3,0,2,1:T(4,128)S(1)}, f32[4,18,1,256]{3,0,2,1:T(4,128)S(1)}, u32[]{:S(2)}, u32[]{:S(2)}) collective-permute-start(f32[4,18,1,256]{3,0,2,1:T(4,128)S(1)} %copy.851), channel_id=1, source_target_pairs={{0,2},{2,4},{4,6},{6,8},{8,10},{10,12},{12,14},{14,0},{1,3},{3,5},... | collective-permute-start | bytes 221192 | tf_op jit(solution)/shard_map/ppermute | solution.py:29
  269.0 7.5 %collective-permute-start.8 = (f32[4,18,1,256]{3,0,2,1:T(4,128)S(1)}, f32[4,18,1,256]{3,0,2,1:T(4,128)S(1)}, u32[]{:S(2)}, u32[]{:S(2)}) collective-permute-start(f32[4,18,1,256]{3,0,2,1:T(4,128)S(1)} %copy.852), channel_id=1, source_target_pairs={{2,0},{4,2},{6,4},{8,6},{10,8},{12,10},{14,12},{0,14},{3,1},{5,3},... | collective-permute-start | bytes 221192 | tf_op jit(solution)/shard_map/ppermute | solution.py:31
  272.4 4.2 %copy-start.14 = (f32[17]{0:T(128)S(1)}, f32[17]{0:T(128)}, u32[]{:S(2)}) copy-start(f32[17]{0:T(128)} %copy-done.13) | copy-start | bytes 208
  276.9 3.7 %copy-start.1 = (bf16[128,128]{1,0:T(8,128)(2,1)S(1)}, bf16[128,128]{1,0:T(8,128)(2,1)}, u32[]{:S(2)}) copy-start(bf16[128,128]{1,0:T(8,128)(2,1)} %param.13) | copy-start | bytes 98308
Sparse Core Ops, SparseCore 0:
  26.7 35.2 reduce-scatter.1
where the time goes:
time: 289 us; the launch traced here: 287 us
  blocking collectives  99 us (34%)
  local copies, waits for them, and re-layouts  89.4 us (31%)
  starting transfers between devices  46.3 us (16%)
  other arithmetic  32.7 us (11%)
  between operations  14.8 us (5%)
  waiting for transfers between devices  4.27 us (1%)
    all_gather x2, blocking collectives, interface_ghost(): picked = lax.all_gather(across, 'pitch', axis=1, tiled=True)  99 us
    unnamed x53, local copies, waits for them, and re-layouts  24.7 us
    ppermute x4, starting transfers between devices, padded(): lax.ppermute(head, axis, [((i + 1) % count, i) for i in range(count)])  21.3 us
    gather x1, local copies, waits for them, and re-layouts, local(): jnp.take(fields.reshape(fields.shape[0], -1), tracer_cells, axis=1)  18.2 us
    ppermute x4, starting transfers between devices, padded(): lax.ppermute(tail, axis, [(i, (i + 1) % count) for i in range(count)])  15.9 us
    another operation x3, other arithmetic  9.41 us
    gather x1, local copies, waits for them, and re-layouts, local(): jnp.take(jnp.stack([speed_axial, speed_pitch]).reshape(2, plane_size), tr...  7.6 us
    scatter x1, local copies, waits for them, and re-layouts, local(): outgoing = jnp.zeros((tracer_values.shape[0], npitch * capacity), jnp.flo...  6.46 us
  transfers between devices with their start and end apart: 12, of which 2 were waited for; matrix products, arithmetic and copies ran while one was open for 39% of the time, Pallas kernels for 0%

commit v1 on v0

--- a/solution.py
+++ b/solution.py
@@ -7,6 +7,11 @@
 TIME_STEP = 0.9
 AXIAL_SPEED = 0.15
 PITCH_SPEED = 0.15
+
+
+def tiled_gather(value, axis, dim):
+    copies = jnp.concatenate([value] * lax.axis_size(axis), axis=dim)
+    return lax.all_to_all(copies, axis, dim, dim, tiled=True)
 
 
 def swapped(block, axis, apart):
@@ -48,7 +53,7 @@
 
 def interface_ghost(own_face, local_map):
     across = swapped(own_face, "row", 0)
-    picked = lax.all_gather(across, "pitch", axis=1, tiled=True)
+    picked = tiled_gather(across, "pitch", 1)
     return jnp.take(picked, local_map, axis=1)
 
 

time: 289 us -> 223 us (0.77)
  the two profiles are of different devices: /device:TPU:24 before, /device:TPU:30 now
where the time goes in v1:
time: 223 us; the launch traced here: 221 us
  local copies, waits for them, and re-layouts  94.5 us (42%)
  starting transfers between devices  58.4 us (26%)
  other arithmetic  35.1 us (16%)
  waiting for transfers between devices  17 us (8%)
  between operations  15.4 us (7%)
    unnamed x125, local copies, waits for them, and re-layouts  35.9 us
    gather x1, local copies, waits for them, and re-layouts, local(): jnp.take(fields.reshape(fields.shape[0], -1), tracer_cells, axis=1)  18.2 us
    ppermute x4, starting transfers between devices, padded(): lax.ppermute(head, axis, [((i + 1) % count, i) for i in range(count)])  17.5 us
    ppermute x4, starting transfers between devices, padded(): lax.ppermute(tail, axis, [(i, (i + 1) % count) for i in range(count)])  16.6 us
    all_to_all x2, starting transfers between devices, tiled_gather(): return lax.all_to_all(copies, axis, dim, dim, tiled=True)  13.1 us
    all_to_all x1, waiting for transfers between devices, local(): lax.all_to_all(outgoing, 'pitch', split_axis=1, concat_axis=1, tiled=True)  9.6 us
    another operation x3, other arithmetic  9.41 us
    gather x1, local copies, waits for them, and re-layouts, local(): jnp.take(jnp.stack([speed_axial, speed_pitch]).reshape(2, plane_size), tr...  7.6 us
  transfers between devices with their start and end apart: 14, of which 4 were waited for; matrix products, arithmetic and copies ran while one was open for 41% of the time, Pallas kernels for 0%

profile of v1, /device:TPU:30, one launch (start us, length us, event | category | flops | bytes accessed | tf_op | source)
XLA Modules:
  0.0 221.2 jit_solution(11641126282921251363)
XLA Ops:
  7.2 1.2 copy.1022
  8.4 1.2 constant_dynamic-update-slice_fusion
  10.5 4.3 %collective-permute-start = (f32[4,1,16,256]{3,2,1,0:T(8,128)}, f32[4,1,16,256]{3,2,1,0:T(8,128)S(1)}, u32[]{:S(2)}, u32[]{:S(2)}) collective-permute-start(f32[4,1,16,256]{3,2,1,0:T(8,128)} %get-tuple-element.57), channel_id=1, source_target_pairs={{0,16},{16,32},{32,48},{48,64},{64,80},{80,96},{96,112},{112,128},... | collective-permute-start | bytes 196616 | tf_op jit(solution)/shard_map/ppermute | solution.py:34
  14.7 8.9 %collective-permute-start.1 = (f32[4,1,16,256]{3,2,1,0:T(8,128)}, f32[4,1,16,256]{3,2,1,0:T(8,128)}, u32[]{:S(2)}, u32[]{:S(2)}) collective-permute-start(f32[4,1,16,256]{3,2,1,0:T(8,128)} %get-tuple-element.58), channel_id=1, source_target_pairs={{16,0},{32,16},{48,32},{64,48},{80,64},{96,80},{112,96},{128,112},... | collective-permute-start | bytes 196616 | tf_op jit(solution)/shard_map/ppermute | solution.py:36
  23.6 0.9 fusion.48
  25.7 16.7 %copy.912 = f32[3,16,16,256]{0,3,2,1:T(8,128)} copy(f32[3,16,16,256]{3,2,1,0:T(8,128)S(1)} %copy-done.2) | data formatting | bytes 1572864 | tf_op args[0]
  42.4 18.2 %gather_fusion = f32[2048,3]{1,0:T(8,128)} fusion(f32[3,65536]{0,1:T(8,128)} %bitcast.125, s32[2048]{0:T(1024)S(1)} %get-tuple-element.74), kind=kCustom, calls=%fused_computation.2 | custom fusion | bytes 57344 | tf_op jit(solution)/shard_map/jit(_take)/gather | solution.py:143
  60.6 2.5 %select_bitcast_fusion.1 = f32[3,2048]{0,1:T(8,128)} fusion(f32[2048,3]{1,0:T(8,128)} %gather_fusion, pred[2048]{0:T(1024)(128)(4,1)S(1)} %get-tuple-element.72), kind=kLoop, calls=%fused_computation.50 | loop fusion | flops 6144 | bytes 51200 | tf_op jit(solution)/shard_map/jit(_take)/select_n | solution.py:143
  63.2 2.2 copy.914
  65.4 9.1 %reduce-window.6 = s32[32,16,128]{2,1,0:T(8,128)S(1)} reduce-window(s32[32,16,128]{2,1,0:T(8,128)S(1)} %fusion.43, s32[]{:T(128)} %constant.30.clone.1), window={size=1x1x128 pad=0_0x0_0x127_0}, to_apply=%region_1.0 | reduce-window | flops 8323072 | bytes 524292 | tf_op jit(solution)/shard_map/reduce-window
  75.9 0.9 pad_maximum_fusion.12
  77.0 4.7 %collective-permute-start.2 = (f32[4,18,1,256]{3,0,2,1:T(4,128)S(1)}, f32[4,18,1,256]{3,0,2,1:T(4,128)S(1)}, u32[]{:S(2)}, u32[]{:S(2)}) collective-permute-start(f32[4,18,1,256]{3,0,2,1:T(4,128)S(1)} %copy.940), channel_id=1, source_target_pairs={{0,2},{2,4},{4,6},{6,8},{8,10},{10,12},{12,14},{14,0},{1,3},{3,5},... | collective-permute-start | bytes 221192 | tf_op jit(solution)/shard_map/ppermute | solution.py:34
  81.7 1.9 collective-permute-start.3
  83.7 2.2 fusion.14
  85.9 0.7 fusion.39
  86.6 0.9 copy.867
  88.3 0.9 collective-permute-done.3
  89.3 1.2 fusion.19
  90.5 0.8 reshape.138
  91.7 0.8 copy.920
  92.6 0.8 copy.921
  94.1 1.9 collective-permute-start.4
  96.8 7.6 %gather_fusion.1 = f32[2048,2]{1,0:T(8,128)} fusion(f32[2,4096]{0,1:T(8,128)S(1)} %copy.913, s32[2048]{0:T(1024)S(1)} %get-tuple-element.75), kind=kCustom, calls=%fused_computation.3 | custom fusion | bytes 40960 | tf_op jit(solution)/shard_map/jit(_take)/gather | solution.py:144
  104.4 1.6 select_bitcast_fusion
  106.4 1.4 copy.916
  107.8 6.5 %scatter_custom_fusion = f32[10,4096]{0,1:T(8,128)S(1)} fusion(s32[2048]{0:T(1024)} %bitcast.149, f32[2048,10]{1,0:T(8,128)} %copy.916, f32[]{:T(128)} %constant.45.clone.1), kind=kCustom, calls=%fused_computation.51 | custom fusion | bytes 164352 | tf_op jit(solution)/shard_map/scatter | solution.py:164
  114.2 1.3 copy.917
  115.6 7.4 %all-to-all-start.2 = ((f32[10,32,128]{2,0,1:T(8,128)}), f32[10,32,128]{2,0,1:T(8,128)}, u32[]{:S(2)}, u32[]{:S(2)}) async-start(f32[10,32,128]{2,0,1:T(8,128)} %copy.917), calls=%async_computation.3 | async-start | bytes 524288 | tf_op jit(solution)/shard_map/all_to_all | solution.py:166
  123.4 1.3 reshape.191
  124.7 9.6 %all-to-all-done.2 = f32[10,32,128]{2,0,1:T(8,128)} async-done(((f32[10,32,128]{2,0,1:T(8,128)}), f32[10,32,128]{2,0,1:T(8,128)}, u32[]{:S(2)}, u32[]{:S(2)}) %all-to-all-start.2) | async-done | bytes 163872 | tf_op jit(solution)/shard_map/all_to_all | solution.py:166
  134.3 6.2 %all-to-all-start = ((f32[32,1,1280]{2,1,0:T(1,128)}), f32[32,1,1280]{2,1,0:T(1,128)S(1)}, u32[]{:S(2)}, u32[]{:S(2)}) async-start(f32[32,1,1280]{2,1,0:T(1,128)} %reshape.191), calls=%async_computation.1 | async-start | bytes 327680 | tf_op jit(solution)/shard_map/all_to_all | solution.py:14
  140.5 2.5 %fusion.5 = f32[3,17,16,256]{3,1,2,0:T(8,128)S(1)} fusion(f32[3,17,16,256]{3,2,1,0:T(8,128)} %get-tuple-element.56, f32[3,17,16,256]{3,2,1,0:T(8,128)} %get-tuple-element.55, f32[17,16,256]{2,0,1:T(8,128)} %copy.867, f32[16,256]{1,0:T(8,128)S(1)} %get-tuple-element.70, f32[16,256]{1,0:T(8,128)S(1)} %get-tuple-element.71), kind=kLoop, calls=%fused_computation.32 | loop fusion | flops 1253376 | bytes 2818048 | tf_op jit(solution)/shard_map/add | solution.py:48
  143.1 1.0 copy.918
  144.1 0.9 copy.951
  145.0 4.1 %all-to-all-done = f32[32,1,1280]{2,1,0:T(1,128)S(1)} async-done(((f32[32,1,1280]{2,1,0:T(1,128)}), f32[32,1,1280]{2,1,0:T(1,128)S(1)}, u32[]{:S(2)}, u32[]{:S(2)}) %all-to-all-start) | async-done | bytes 163872 | tf_op jit(solution)/shard_map/all_to_all | solution.py:14
  149.6 1.0 reduce
  150.6 2.1 reshape.192
  152.7 2.8 %gather_fusion.2 = f32[16,5,16]{2,1,0:T(8,128)} fusion(f32[5,512,16]{2,0,1:T(8,128)} %bitcast.136, s32[1024]{0:T(1024)S(1)} %pad_clamp_fusion), kind=kCustom, calls=%fused_computation.clone | custom fusion | bytes 10304 | tf_op jit(solution)/shard_map/jit(_take)/gather | solution.py:57
  155.5 1.0 fusion.46
  156.4 1.4 copy.882
  157.8 1.4 copy.885
  159.2 2.0 fusion.2
  161.6 0.9 copy-done.5
  162.5 0.8 fusion.23
  164.1 1.0 fusion.60
  165.1 1.9 copy.928
  167.1 0.8 copy.929
  167.9 1.9 collective-permute-start.9
  169.9 3.4 %collective-permute-start.5 = (f32[4,1,16,256]{3,2,1,0:T(8,128)S(1)}, f32[4,1,16,256]{3,2,1,0:T(8,128)S(1)}, u32[]{:S(2)}, u32[]{:S(2)}) collective-permute-start(f32[4,1,16,256]{3,2,1,0:T(8,128)S(1)} %get-tuple-element.53), channel_id=1, source_target_pairs={{0,16},{16,32},{32,48},{48,64},{64,80},{80,96},{96,112},{112,128},... | collective-permute-start | bytes 196616 | tf_op jit(solution)/shard_map/ppermute | solution.py:34
  173.3 4.6 %collective-permute-start.6 = (f32[4,1,16,256]{3,2,1,0:T(8,128)S(1)}, f32[4,1,16,256]{3,2,1,0:T(8,128)S(1)}, u32[]{:S(2)}, u32[]{:S(2)}) collective-permute-start(f32[4,1,16,256]{3,2,1,0:T(8,128)S(1)} %get-tuple-element.54), channel_id=1, source_target_pairs={{16,0},{32,16},{48,32},{64,48},{80,64},{96,80},{112,96},{128,112},... | collective-permute-start | bytes 196616 | tf_op jit(solution)/shard_map/ppermute | solution.py:36
  178.3 1.3 copy-done.7
  179.7 2.9 %reshape.193 = f32[32,1,1280]{2,1,0:T(1,128)} reshape(f32[512,5,16]{2,1,0:T(8,128)} %bitcast.134) | data formatting | bytes 327680
  182.6 6.9 %all-to-all-start.1 = ((f32[32,1,1280]{2,1,0:T(1,128)}), f32[32,1,1280]{2,1,0:T(1,128)S(1)}, u32[]{:S(2)}, u32[]{:S(2)}) async-start(f32[32,1,1280]{2,1,0:T(1,128)} %reshape.193), calls=%async_computation.2 | async-start | bytes 327680 | tf_op jit(solution)/shard_map/all_to_all | solution.py:14
  190.0 4.2 %collective-permute-start.7 = (f32[4,18,1,256]{3,0,2,1:T(4,128)S(1)}, f32[4,18,1,256]{3,0,2,1:T(4,128)S(1)}, u32[]{:S(2)}, u32[]{:S(2)}) collective-permute-start(f32[4,18,1,256]{3,0,2,1:T(4,128)S(1)} %copy.945), channel_id=1, source_target_pairs={{0,2},{2,4},{4,6},{6,8},{8,10},{10,12},{12,14},{14,0},{1,3},{3,5},... | collective-permute-start | bytes 221192 | tf_op jit(solution)/shard_map/ppermute | solution.py:34
  194.3 2.1 collective-permute-start.8
  196.6 2.0 fusion.8
  199.4 2.3 %collective-permute-done.8 = f32[4,18,1,256]{3,0,2,1:T(4,128)S(1)} collective-permute-done((f32[4,18,1,256]{3,0,2,1:T(4,128)S(1)}, f32[4,18,1,256]{3,0,2,1:T(4,128)S(1)}, u32[]{:S(2)}, u32[]{:S(2)}) %collective-permute-start.8) | collective-permute-done | bytes 73760 | tf_op jit(solution)/shard_map/ppermute | solution.py:36
  202.1 1.0 reduce.1
  203.1 2.1 reshape.194
  205.2 2.1 gather_fusion.3
  208.0 1.4 copy.908
  209.4 1.8 fusion.3
  211.5 1.0 copy-done.6
  213.1 1.3 copy.919
  (177 shorter events, 12.0 us)
Async XLA Ops:
  7.2 16.5 %copy-start = (bf16[128,128]{1,0:T(8,128)(2,1)S(1)}, bf16[128,128]{1,0:T(8,128)(2,1)}, u32[]{:S(2)}) copy-start(bf16[128,128]{1,0:T(8,128)(2,1)} %param.13) | copy-start | bytes 98308
  7.2 17.4 %copy-start.2 = (f32[3,16,16,256]{3,2,1,0:T(8,128)S(1)}, f32[3,16,16,256]{3,2,1,0:T(8,128)}, u32[]{:S(2)}) copy-start(f32[3,16,16,256]{3,2,1,0:T(8,128)} %param.10) | copy-start | bytes 2359300
  7.2 16.4 %copy-start.15 = (bf16[16,2,256]{2,1,0:T(2,128)(2,1)S(1)}, bf16[16,2,256]{2,1,0:T(2,128)(2,1)}, u32[]{:S(2)}) copy-start(bf16[16,2,256]{2,1,0:T(2,128)(2,1)} %param.12) | copy-start | bytes 49156
  7.2 83.3 %reduce-scatter.2.cloned.1.call-start = ((), (), s32[]{:S(2)}) async-start(), calls=%async_computation.4 | async-start | bytes 294912 | tf_op jit(solution)/shard_map/reduce_scatter | solution.py:133
  8.4 16.7 %copy-start.19 = (s32[1,16]{1,0:T(1,128)S(1)}, s32[1,16]{1,0:T(1,128)}, u32[]{:S(2)}) copy-start(s32[1,16]{1,0:T(1,128)} %param.17) | copy-start | bytes 196
  8.4 17.2 %copy-start.14 = (s32[2048]{0:T(1024)S(1)}, s32[2048]{0:T(1024)}, u32[]{:S(2)}) copy-start(s32[2048]{0:T(1024)} %param.15) | copy-start | bytes 24580
  10.5 65.5 %collective-permute-start = (f32[4,1,16,256]{3,2,1,0:T(8,128)}, f32[4,1,16,256]{3,2,1,0:T(8,128)S(1)}, u32[]{:S(2)}, u32[]{:S(2)}) collective-permute-start(f32[4,1,16,256]{3,2,1,0:T(8,128)} %get-tuple-element.57), channel_id=1, source_target_pairs={{0,16},{16,32},{32,48},{48,64},{64,80},{80,96},{96,112},{112,128},... | collective-permute-start | bytes 196616 | tf_op jit(solution)/shard_map/ppermute | solution.py:34
  14.7 61.2 %collective-permute-start.1 = (f32[4,1,16,256]{3,2,1,0:T(8,128)}, f32[4,1,16,256]{3,2,1,0:T(8,128)}, u32[]{:S(2)}, u32[]{:S(2)}) collective-permute-start(f32[4,1,16,256]{3,2,1,0:T(8,128)} %get-tuple-element.58), channel_id=1, source_target_pairs={{16,0},{32,16},{48,32},{64,48},{80,64},{96,80},{112,96},{128,112},... | collective-permute-start | bytes 196616 | tf_op jit(solution)/shard_map/ppermute | solution.py:36
  25.1 66.3 %copy-start.3 = (f32[3,16,16,256]{3,1,2,0:T(8,128)}, f32[3,16,16,256]{3,1,2,0:T(8,128)S(1)}, u32[]{:S(2)}) copy-start(f32[3,16,16,256]{3,1,2,0:T(8,128)S(1)} %copy.887) | copy-start | bytes 2359300
  42.4 22.9 %copy-start.13 = (s32[2048,1]{0,1:T(1,128)S(1)}, s32[2048,1]{0,1:T(1,128)}, u32[]{:S(2)}) copy-start(s32[2048,1]{0,1:T(1,128)} %param.16) | copy-start | bytes 24580
  75.9 13.4 %copy-start.17 = (f32[17]{0:T(128)}, f32[17]{0:T(128)S(1)}, u32[]{:S(2)}) copy-start(f32[17]{0:T(128)S(1)} %and_convert_fusion) | copy-start | bytes 208
  77.0 10.5 %collective-permute-start.2 = (f32[4,18,1,256]{3,0,2,1:T(4,128)S(1)}, f32[4,18,1,256]{3,0,2,1:T(4,128)S(1)}, u32[]{:S(2)}, u32[]{:S(2)}) collective-permute-start(f32[4,18,1,256]{3,0,2,1:T(4,128)S(1)} %copy.940), channel_id=1, source_target_pairs={{0,2},{2,4},{4,6},{6,8},{8,10},{10,12},{12,14},{14,0},{1,3},{3,5},... | collective-permute-start | bytes 221192 | tf_op jit(solution)/shard_map/ppermute | solution.py:34
  81.7 7.5 %collective-permute-start.3 = (f32[4,18,1,256]{3,0,2,1:T(4,128)S(1)}, f32[4,18,1,256]{3,0,2,1:T(4,128)S(1)}, u32[]{:S(2)}, u32[]{:S(2)}) collective-permute-start(f32[4,18,1,256]{3,0,2,1:T(4,128)S(1)} %copy.941), channel_id=1, source_target_pairs={{2,0},{4,2},{6,4},{8,6},{10,8},{12,10},{14,12},{0,14},{3,1},{5,3},... | collective-permute-start | bytes 221192 | tf_op jit(solution)/shard_map/ppermute | solution.py:36
  92.6 3.5 %copy-start.8 = (f32[5,16,16,1]{2,0,1,3:T(8,128)}, f32[5,16,16,1]{2,0,1,3:T(8,128)S(1)}, u32[]{:S(2)}) copy-start(f32[5,16,16,1]{2,0,1,3:T(8,128)S(1)} %copy.920) | copy-start | bytes 15364
  93.4 2.7 %copy-start.10 = (f32[5,16,16,1]{2,0,1,3:T(8,128)}, f32[5,16,16,1]{2,0,1,3:T(8,128)S(1)}, u32[]{:S(2)}) copy-start(f32[5,16,16,1]{2,0,1,3:T(8,128)S(1)} %copy.921) | copy-start | bytes 15364
  94.1 28.9 %collective-permute-start.4 = (f32[5,16,16]{2,0,1:T(8,128)}, f32[5,16,16]{2,0,1:T(8,128)S(1)}, u32[]{:S(2)}, u32[]{:S(2)}) collective-permute-start(f32[5,16,16]{2,0,1:T(8,128)} %bitcast_select_fusion.5), channel_id=1, source_target_pairs={{0,1},{1,0},{2,3},{3,2},{4,5},{5,4},{6,7},{7,6},{8,9},{9,8},{10,11... | collective-permute-start | bytes 15368 | tf_op jit(solution)/shard_map/ppermute | solution.py:24
  96.8 9.5 %copy-start.11 = (f32[3,2048]{1,0:T(4,128)S(1)}, f32[3,2048]{1,0:T(4,128)}, u32[]{:S(2)}) copy-start(f32[3,2048]{1,0:T(4,128)} %copy.914) | copy-start | bytes 73732
  104.4 1.9 copy-start.12
  115.6 18.8 %all-to-all-start.2 = ((f32[10,32,128]{2,0,1:T(8,128)}), f32[10,32,128]{2,0,1:T(8,128)}, u32[]{:S(2)}, u32[]{:S(2)}) async-start(f32[10,32,128]{2,0,1:T(8,128)} %copy.917), calls=%async_computation.3 | async-start | bytes 524288 | tf_op jit(solution)/shard_map/all_to_all | solution.py:166
  134.3 14.7 %all-to-all-start = ((f32[32,1,1280]{2,1,0:T(1,128)}), f32[32,1,1280]{2,1,0:T(1,128)S(1)}, u32[]{:S(2)}, u32[]{:S(2)}) async-start(f32[32,1,1280]{2,1,0:T(1,128)} %reshape.191), calls=%async_computation.1 | async-start | bytes 327680 | tf_op jit(solution)/shard_map/all_to_all | solution.py:14
  143.0 12.4 %copy-start.9 = (f32[5,16,16,1]{2,0,1,3:T(8,128)S(1)}, f32[5,16,16,1]{2,0,1,3:T(8,128)}, u32[]{:S(2)}) copy-start(f32[5,16,16,1]{2,0,1,3:T(8,128)} %copy-done.8) | copy-start | bytes 15364
  143.0 12.4 %copy-start.16 = (pred[16]{0:T(512)(128)(4,1)S(1)}, pred[16]{0:T(512)(128)(4,1)}, u32[]{:S(2)}) copy-start(pred[16]{0:T(512)(128)(4,1)} %compare_and_fusion.2) | copy-start | bytes 52
  150.6 8.6 %copy-start.4 = (f32[3,16,16,256]{3,1,2,0:T(8,128)S(1)}, f32[3,16,16,256]{3,1,2,0:T(8,128)}, u32[]{:S(2)}) copy-start(f32[3,16,16,256]{3,1,2,0:T(8,128)} %copy-done.3) | copy-start | bytes 2359300
  161.3 1.2 copy-start.5
  167.9 9.9 %collective-permute-start.9 = (f32[5,16,16]{2,0,1:T(8,128)S(1)}, f32[5,16,16]{2,0,1:T(8,128)S(1)}, u32[]{:S(2)}, u32[]{:S(2)}) collective-permute-start(f32[5,16,16]{2,0,1:T(8,128)S(1)} %bitcast_select_fusion.2), channel_id=1, source_target_pairs={{0,1},{1,0},{2,3},{3,2},{4,5},{5,4},{6,7},{7,6},{8,9},{9,8},{10,11... | collective-permute-start | bytes 15368 | tf_op jit(solution)/shard_map/ppermute | solution.py:24
  169.9 19.7 %collective-permute-start.5 = (f32[4,1,16,256]{3,2,1,0:T(8,128)S(1)}, f32[4,1,16,256]{3,2,1,0:T(8,128)S(1)}, u32[]{:S(2)}, u32[]{:S(2)}) collective-permute-start(f32[4,1,16,256]{3,2,1,0:T(8,128)S(1)} %get-tuple-element.53), channel_id=1, source_target_pairs={{0,16},{16,32},{32,48},{48,64},{64,80},{80,96},{96,112},{112,128},... | collective-permute-start | bytes 196616 | tf_op jit(solution)/shard_map/ppermute | solution.py:34
  173.3 16.3 %collective-permute-start.6 = (f32[4,1,16,256]{3,2,1,0:T(8,128)S(1)}, f32[4,1,16,256]{3,2,1,0:T(8,128)S(1)}, u32[]{:S(2)}, u32[]{:S(2)}) collective-permute-start(f32[4,1,16,256]{3,2,1,0:T(8,128)S(1)} %get-tuple-element.54), channel_id=1, source_target_pairs={{16,0},{32,16},{48,32},{64,48},{80,64},{96,80},{112,96},{128,112},... | collective-permute-start | bytes 196616 | tf_op jit(solution)/shard_map/ppermute | solution.py:36
  178.3 1.4 copy-start.7
  182.6 19.5 %all-to-all-start.1 = ((f32[32,1,1280]{2,1,0:T(1,128)}), f32[32,1,1280]{2,1,0:T(1,128)S(1)}, u32[]{:S(2)}, u32[]{:S(2)}) async-start(f32[32,1,1280]{2,1,0:T(1,128)} %reshape.193), calls=%async_computation.2 | async-start | bytes 327680 | tf_op jit(solution)/shard_map/all_to_all | solution.py:14
  190.0 8.7 %collective-permute-start.7 = (f32[4,18,1,256]{3,0,2,1:T(4,128)S(1)}, f32[4,18,1,256]{3,0,2,1:T(4,128)S(1)}, u32[]{:S(2)}, u32[]{:S(2)}) collective-permute-start(f32[4,18,1,256]{3,0,2,1:T(4,128)S(1)} %copy.945), channel_id=1, source_target_pairs={{0,2},{2,4},{4,6},{6,8},{8,10},{10,12},{12,14},{14,0},{1,3},{3,5},... | collective-permute-start | bytes 221192 | tf_op jit(solution)/shard_map/ppermute | solution.py:34
  194.3 7.5 %collective-permute-start.8 = (f32[4,18,1,256]{3,0,2,1:T(4,128)S(1)}, f32[4,18,1,256]{3,0,2,1:T(4,128)S(1)}, u32[]{:S(2)}, u32[]{:S(2)}) collective-permute-start(f32[4,18,1,256]{3,0,2,1:T(4,128)S(1)} %copy.946), channel_id=1, source_target_pairs={{2,0},{4,2},{6,4},{8,6},{10,8},{12,10},{14,12},{0,14},{3,1},{5,3},... | collective-permute-start | bytes 221192 | tf_op jit(solution)/shard_map/ppermute | solution.py:36
  198.7 3.1 %copy-start.18 = (f32[17]{0:T(128)S(1)}, f32[17]{0:T(128)}, u32[]{:S(2)}) copy-start(f32[17]{0:T(128)} %copy-done.17) | copy-start | bytes 208
  211.3 1.3 copy-start.6
  212.6 1.8 copy-start.1
Sparse Core Ops, SparseCore 0:
  24.7 37.1 reduce-scatter.1
